TPU v7x, 256 devices: a whole 4x4x8 slice. The times are simulated.
256 devices in a mesh: seq: 64 (over z, x, core), tp: 4 (over y).
Axes of the slice: x: 4, y: 4, z: 8, core: 2. Of those that a mesh axis runs over, the one named last changes fastest.
Arguments:
- tokens: bfloat16 [32768, 2048], P('seq', 'tp'), may hold values from -6 to 6
- norm_gain: float32 [2048], replicated, may hold values from 0.1 to 1.9
- w_query: bfloat16 [2048, 2048], P(None, 'tp'), may hold values from -0.125 to 0.125
- w_keyval: bfloat16 [2048, 256], replicated, may hold values from -0.125 to 0.125
- w_out: bfloat16 [2048, 2048], P('tp'), may hold values from -0.5 to 0.5
- span_lens: int32 [64], P('seq'), may hold values from 1 to 512, 24576 in all
- cached_lens: int32 [64], P('seq'), may hold values from 1 to 1536, 49152 in all
- old_table: int32 [64, 64], P('seq'), may hold values from 0 to 63, each once within a row
- new_table: int32 [64, 64], P('seq'), may hold values from 0 to 63, each once within a row
- old_cache: bfloat16 [4096, 32, 256], P('seq', 'tp'), may hold values from -720 to 720
Outputs:
- mixed: bfloat16 [32768, 2048], P('seq', 'tp')
- new_cache: bfloat16 [4096, 32, 256], P('seq', 'tp')
Inputs may be any that keep to these rules, and one draw needn't show every extreme that they name: Request r's new tokens are the first span_lens[r] of its 512 rows. `old_table`: each row names every device once: each device holds exactly one block of every request. `new_table`: each row names every device once: each device receives exactly one block of every request.
All inputs are finite; a program needn't handle non-finite values. No bound on the sum of `span_lens` or of `cached_lens` on one device may be relied on, other than what follows from the above.
Results may differ from a plain program's by a relative error of at most 0.012.
The roundings to bfloat16 on the way count: a program that leaves them out, or rounds other values in their place, can miss the bound.
Values may be sent and summed in bfloat16 or wider, within the bound.
A program may use at most 128 MiB of HBM per device.

v0:
```python
import jax
import jax.numpy as jnp
from jax import lax
from jax.sharding import PartitionSpec as P

EPSILON = 1e-05
MASKED = -1e30


def normalize(rows, norm_gain):
    values = rows.astype(jnp.float32)
    average = jnp.mean(values, axis=1, keepdims=True)
    centred = values - average
    spread = jnp.mean(centred * centred, axis=1, keepdims=True)
    return (centred * lax.rsqrt(spread + EPSILON) * norm_gain).astype(jnp.bfloat16)


def body(
    tokens,
    norm_gain,
    w_query,
    w_keyval,
    w_out,
    span_lens,
    cached_lens,
    old_table,
    new_table,
    old_cache,
):
    full_rows = lax.all_gather(tokens, "tp", axis=1, tiled=True)
    normed = normalize(full_rows, norm_gain)
    query = jnp.dot(normed, w_query, preferred_element_type=jnp.float32).astype(jnp.bfloat16)
    keyval = jnp.dot(normed, w_keyval, preferred_element_type=jnp.float32).astype(jnp.bfloat16)
    groups = lax.axis_size("seq")
    tp_count = lax.axis_size("tp")
    holders = old_table[0]
    pooled = lax.all_gather(old_cache, "tp", axis=1, tiled=True)
    arrived = lax.all_to_all(pooled, "seq", split_axis=0, concat_axis=0, tiled=True)
    ordered = jnp.take(arrived, holders, axis=0)
    block_rows = ordered.shape[1]
    width = ordered.shape[2]
    capacity = groups * block_rows
    cached = ordered.reshape(capacity, width)
    held_len = cached_lens[0]
    span_len = span_lens[0]
    tok_rows = tokens.shape[0]
    share = block_rows // tp_count
    targets = new_table[0]
    device_ids = lax.broadcasted_iota(jnp.int32, (groups, groups), 0)
    block_ids = lax.broadcasted_iota(jnp.int32, (groups, groups), 1)
    matches = targets[None, :] == device_ids
    sources = jnp.sum(jnp.where(matches, block_ids, 0), axis=1)
    positions = lax.broadcasted_iota(jnp.int32, (capacity, 1), 0)
    placed = lax.dynamic_update_slice(cached, keyval, (held_len, jnp.int32(0)))
    fresh = jnp.where(positions < held_len + span_len, placed, jnp.zeros_like(placed))
    head_size = width // 2
    keys = fresh[:, :head_size]
    values = fresh[:, head_size:]
    local_heads = query.shape[1] // head_size
    query3 = query.reshape(tok_rows, local_heads, head_size)
    scores = jnp.einsum(
        "thd,kd->htk", query3, keys, preferred_element_type=jnp.float32
    ) * head_size ** (-0.5)
    row_pos = lax.broadcasted_iota(jnp.int32, (tok_rows, 1), 0)
    key_pos = lax.broadcasted_iota(jnp.int32, (1, capacity), 1)
    allowed = key_pos <= held_len + row_pos
    scores = jnp.where(allowed[None], scores, MASKED)
    top = jnp.max(scores, axis=2, keepdims=True)
    weights = jnp.exp(scores - top)
    probs = (weights / jnp.sum(weights, axis=2, keepdims=True)).astype(jnp.bfloat16)
    context = jnp.einsum("htk,kd->thd", probs, values, preferred_element_type=jnp.float32).astype(
        jnp.bfloat16
    )
    context = context.reshape(tok_rows, local_heads * head_size)
    partial_out = jnp.dot(context, w_out, preferred_element_type=jnp.float32)
    summed = lax.psum_scatter(
        partial_out.astype(jnp.bfloat16), "tp", scatter_dimension=1, tiled=True
    ).astype(jnp.float32)
    total = tokens.astype(jnp.float32) + summed
    mixed = jnp.where(row_pos < span_len, total, jnp.zeros_like(total)).astype(jnp.bfloat16)
    mine_part = lax.dynamic_slice_in_dim(
        fresh.reshape(groups, block_rows, width), lax.axis_index("tp") * share, share, 1
    )
    new_cache = lax.all_to_all(
        jnp.take(mine_part, sources, axis=0), "seq", split_axis=0, concat_axis=0, tiled=True
    )
    return (mixed, new_cache)


def solution(mesh):
    in_specs = (
        P("seq", "tp"),
        P(),
        P(None, "tp"),
        P(),
        P("tp", None),
        P("seq"),
        P("seq"),
        P("seq", None),
        P("seq", None),
        P("seq", "tp", None),
    )
    out_specs = (P("seq", "tp"), P("seq", "tp", None))
    return jax.shard_map(body, mesh=mesh, in_specs=in_specs, out_specs=out_specs, check_vma=False)
```

profile of v0, /device:TPU:1, one launch (start us, length us, event | category | flops | bytes accessed | tf_op | source)
XLA Modules:
  0.0 154.8 jit_solution(5848110831717273681)
XLA Ops:
  7.2 0.0 copy-start
  7.2 0.0 copy-start.4
  7.2 0.0 all-gather.3.cloned.1.call-start
  7.2 0.7 all-gather.3.cloned.1.call-update
  7.9 0.0 all-gather.5.cloned.1.call-start
  8.0 0.7 all-gather.5.cloned.1.call-update
  9.3 0.7 compare_and_fusion.1
  10.0 0.1 broadcast_in_dim.70
  10.1 0.1 broadcast_in_dim.71
  10.8 0.7 fusion.15
  11.5 1.8 %iota_compare_fusion = pred[512,2048]{0,1:T(8,128)(4,1)} fusion(s32[512]{0:T(512)S(1)} %iota_add_fusion), kind=kLoop, calls=%fused_computation.18 | loop fusion | flops 1048576 | bytes 1050624 | tf_op jit(solution)/shard_map/le | solution.py:66
  13.3 27.9 %all-gather.3.cloned.1.call-done = bf16[64,32,256]{2,1,0:T(8,128)(2,1)} async-done(((bf16[64,8,256]{2,1,0:T(8,128)(2,1)}), bf16[64,32,256]{2,1,0:T(8,128)(2,1)}) %all-gather.3.cloned.1.call-update) | async-done | bytes 1048592 | tf_op jit(solution)/shard_map/all_gather | solution.py:37
  41.2 11.5 %all-to-all-start = ((bf16[64,32,256]{2,1,0:T(8,128)(2,1)}), bf16[64,32,256]{2,1,0:T(8,128)(2,1)S(1)}, u32[]{:S(2)}, u32[]{:S(2)}) async-start(bf16[64,32,256]{2,1,0:T(8,128)(2,1)} %all-gather.3.cloned.1.call-done), calls=%async_computation | async-start | bytes 2097152 | tf_op jit(solution)/shard_map/all_to_all | solution.py:38
  52.8 0.0 reduce-scatter.2.cloned.1.call-start
  52.8 25.5 %all-gather.5.cloned.1.call-done = bf16[512,2048]{1,0:T(8,128)(2,1)} async-done(((bf16[512,512]{1,0:T(8,128)(2,1)}), bf16[512,2048]{1,0:T(8,128)(2,1)}) %all-gather.5.cloned.1.call-update) | async-done | bytes 2097168 | tf_op jit(solution)/shard_map/all_gather | solution.py:30
  78.3 2.1 %convert_reduce_fusion = f32[512]{0:T(512)S(1)} fusion(bf16[512,2048]{1,0:T(8,128)(2,1)} %all-gather.5.cloned.1.call-done), kind=kLoop, calls=%fused_computation.12 | loop fusion | flops 2096640 | bytes 2099200 | tf_op jit(solution)/shard_map/reduce_sum | solution.py:12
  80.4 2.3 %fusion.8 = f32[512]{0:T(512)S(1)} fusion(bf16[512,2048]{1,0:T(8,128)(2,1)} %all-gather.5.cloned.1.call-done, f32[512]{0:T(512)S(1)} %broadcast_multiply_fusion), kind=kLoop, calls=%fused_computation.15 | loop fusion | flops 4193792 | bytes 2101248 | tf_op jit(solution)/shard_map/reduce_sum | solution.py:14
  82.7 0.0 copy-done.4
  82.8 0.0 copy-done.1
  82.8 0.7 fusion.10
  83.5 0.0 copy-done.6
  83.5 0.7 convolution_convert_fusion.2
  84.2 0.1 copy-done.5
  84.3 2.1 %convolution_convert_fusion.1 = bf16[512,512]{0,1:T(8,128)(2,1)} fusion(bf16[512,2048]{1,0:T(8,128)(2,1)S(1)} %fusion.10, bf16[2048,512]{1,0:T(8,128)(2,1)S(1)} %copy-done.5), kind=kOutput, calls=%fused_computation.21 | convolution fusion | flops 1074003968 | bytes 4718592 | tf_op jit(solution)/shard_map/dot_general | solution.py:32
  86.4 0.0 all-to-all-done
  86.4 1.6 %gather_fusion = bf16[64,32,256]{2,1,0:T(8,128)(2,1)} fusion(bf16[64,32,256]{2,1,0:T(8,128)(2,1)S(1)} %all-to-all-done, s32[1024]{0:T(1024)S(1)} %pad_clamp_fusion.1), kind=kCustom, calls=%fused_computation | custom fusion | bytes 2097408 | tf_op jit(solution)/shard_map/jit(_take)/gather | solution.py:39
  88.0 1.5 bitcast_select_fusion.4
  89.5 1.9 %dynamic_update_slice.3 = bf16[2048,256]{1,0:T(8,128)(2,1)S(1)} dynamic-update-slice(bf16[2048,256]{1,0:T(8,128)(2,1)S(1)} %bitcast_select_fusion.4, bf16[512,256]{1,0:T(8,128)(2,1)S(1)} %convolution_convert_fusion.2, s32[]{:T(128)S(6)} %select_n.65, s32[]{:T(128)} %constant.15.clone.1) | dynamic-update-slice | bytes 524292 | tf_op jit(solution)/shard_map/dynamic_update_slice | solution.py:54
  91.4 1.2 broadcast_select_fusion
  92.6 10.7 %fusion.19 = (f32[4,512]{1,0:T(4,128)S(1)}, f32[4,512,2048]{1,2,0:T(8,128)}) fusion(pred[512,2048]{0,1:T(8,128)(4,1)} %iota_compare_fusion, bf16[512,4,128]{0,2,1:T(8,128)(2,1)} %bitcast.63, bf16[2048,256]{1,0:T(8,128)(2,1)} %broadcast_select_fusion), kind=kOutput, calls=%fused_computation.51 | convolution fusion | flops 1090521088 | bytes 18882560 | tf_op jit(solution)/shard_map/sub | solution.py:69
  103.3 0.0 copy-done.3
  103.4 7.0 %fusion.13 = bf16[128,4,512]{2,0,1:T(8,128)(2,1)S(1)} fusion(f32[4,512,2048]{1,2,0:T(8,128)} %get-tuple-element.3, f32[4,512]{1,0:T(4,128)S(1)} %get-tuple-element.2, bf16[2048,256]{1,0:T(8,128)(2,1)S(1)} %copy-done.3), kind=kOutput, calls=%fused_computation.22 | convolution fusion | flops 1082392576 | bytes 17833984 | tf_op jit(solution)/shard_map/htk,kd->thd/dot_general | solution.py:71
  110.4 0.0 copy-start.7
  110.4 0.0 copy-done
  110.4 0.0 copy-start.2
  110.4 2.6 %convolution_convert_fusion = bf16[512,2048]{1,0:T(8,128)(2,1)} fusion(bf16[512,512]{0,1:T(8,128)(2,1)S(1)} %bitcast.64, bf16[512,2048]{1,0:T(8,128)(2,1)S(1)} %copy-done), kind=kOutput, calls=%fused_computation.19 | convolution fusion | flops 1074790400 | bytes 4718592 | tf_op jit(solution)/shard_map/dot_general | solution.py:75
  113.1 0.0 reduce-scatter.2.cloned.1.call-update
  113.1 0.0 copy-done.7
  113.1 0.1 select_reduce_fusion
  113.2 1.0 constant_dynamic-slice_fusion
  114.2 0.6 gather_fusion.1
  114.8 0.8 broadcast_select_fusion.1
  115.7 10.6 %all-to-all-start.1 = ((bf16[64,8,256]{2,1,0:T(8,128)(2,1)}), bf16[64,8,256]{2,1,0:T(8,128)(2,1)S(1)}, u32[]{:S(2)}, u32[]{:S(2)}) async-start(bf16[64,8,256]{2,1,0:T(8,128)(2,1)} %broadcast_select_fusion.1), calls=%async_computation.2 | async-start | bytes 524288 | tf_op jit(solution)/shard_map/all_to_all | solution.py:84
  126.3 13.1 %all-to-all-done.1 = bf16[64,8,256]{2,1,0:T(8,128)(2,1)S(1)} async-done(((bf16[64,8,256]{2,1,0:T(8,128)(2,1)}), bf16[64,8,256]{2,1,0:T(8,128)(2,1)S(1)}, u32[]{:S(2)}, u32[]{:S(2)}) %all-to-all-start.1) | async-done | bytes 262176 | tf_op jit(solution)/shard_map/all_to_all | solution.py:84
  139.5 6.1 %reduce-scatter.2.cloned.1.call-done = bf16[512,512]{1,0:T(8,128)(2,1)} async-done(((bf16[512,2048]{1,0:T(8,128)(2,1)}), bf16[512,512]{1,0:T(8,128)(2,1)}) %reduce-scatter.2.cloned.1.call-update) | async-done | bytes 524304 | tf_op jit(solution)/shard_map/reduce_scatter | solution.py:76
  145.6 0.0 copy-done.2
  145.6 2.0 %select_convert_fusion = bf16[512,512]{1,0:T(8,128)(2,1)} fusion(bf16[512,512]{1,0:T(8,128)(2,1)} %reduce-scatter.2.cloned.1.call-done, bf16[512,512]{1,0:T(8,128)(2,1)S(1)} %copy-done.2, pred[512]{0:T(512)(128)(4,1)S(1)} %iota_compare_fusion.3), kind=kLoop, calls=%fused_computation.25 | loop fusion | flops 1310720 | bytes 1573376 | tf_op jit(solution)/shard_map/convert_element_type | solution.py:80
  147.6 0.7 copy.29
  (13 shorter events, 0.1 us)
Async XLA Ops:
  7.2 103.3 %copy-start = (bf16[512,2048]{1,0:T(8,128)(2,1)S(1)}, bf16[512,2048]{1,0:T(8,128)(2,1)}, u32[]{:S(2)}) copy-start(bf16[512,2048]{1,0:T(8,128)(2,1)} %param.14) | copy-start | bytes 6291460
  7.2 75.6 %copy-start.4 = (f32[2048]{0:T(1024)S(1)}, f32[2048]{0:T(1024)}, u32[]{:S(2)}) copy-start(f32[2048]{0:T(1024)} %param.11) | copy-start | bytes 24580
  7.2 34.0 %all-gather.3.cloned.1.call-start = ((), (), s32[]{:S(2)}) async-start(), calls=%async_computation.3 | async-start | bytes 1310720 | tf_op jit(solution)/shard_map/all_gather | solution.py:37
  7.9 70.4 %all-gather.5.cloned.1.call-start = ((), (), s32[]{:S(2)}) async-start(), calls=%async_computation.4 | async-start | bytes 2621440 | tf_op jit(solution)/shard_map/all_gather | solution.py:30
  41.2 45.2 %all-to-all-start = ((bf16[64,32,256]{2,1,0:T(8,128)(2,1)}), bf16[64,32,256]{2,1,0:T(8,128)(2,1)S(1)}, u32[]{:S(2)}, u32[]{:S(2)}) async-start(bf16[64,32,256]{2,1,0:T(8,128)(2,1)} %all-gather.3.cloned.1.call-done), calls=%async_computation | async-start | bytes 2097152 | tf_op jit(solution)/shard_map/all_to_all | solution.py:38
  52.8 92.8 %reduce-scatter.2.cloned.1.call-start = ((), (), s32[]{:S(2)}) async-start(), calls=%async_computation.5 | async-start | bytes 2621440 | tf_op jit(solution)/shard_map/reduce_scatter | solution.py:76
  78.3 4.4 %copy-start.1 = (bf16[512,2048]{1,0:T(8,128)(2,1)S(1)}, bf16[512,2048]{1,0:T(8,128)(2,1)}, u32[]{:S(2)}) copy-start(bf16[512,2048]{1,0:T(8,128)(2,1)} %all-gather.5.cloned.1.call-done) | copy-start | bytes 6291460
  78.3 5.1 %copy-start.6 = (bf16[2048,256]{1,0:T(8,128)(2,1)S(1)}, bf16[2048,256]{1,0:T(8,128)(2,1)}, u32[]{:S(2)}) copy-start(bf16[2048,256]{1,0:T(8,128)(2,1)} %param.13) | copy-start | bytes 3145732
  82.7 1.6 %copy-start.5 = (bf16[2048,512]{1,0:T(8,128)(2,1)S(1)}, bf16[2048,512]{1,0:T(8,128)(2,1)}, u32[]{:S(2)}) copy-start(bf16[2048,512]{1,0:T(8,128)(2,1)} %param.12) | copy-start | bytes 6291460
  92.6 10.7 %copy-start.3 = (bf16[2048,256]{1,0:T(8,128)(2,1)S(1)}, bf16[2048,256]{1,0:T(8,128)(2,1)}, u32[]{:S(2)}) copy-start(bf16[2048,256]{1,0:T(8,128)(2,1)} %broadcast_select_fusion) | copy-start | bytes 3145732
  110.4 2.7 %copy-start.7 = (s32[1,64]{1,0:T(1,128)S(1)}, s32[1,64]{1,0:T(1,128)}, u32[]{:S(2)}) copy-start(s32[1,64]{1,0:T(1,128)} %param.18) | copy-start | bytes 772
  110.4 35.1 %copy-start.2 = (bf16[512,512]{1,0:T(8,128)(2,1)S(1)}, bf16[512,512]{1,0:T(8,128)(2,1)}, u32[]{:S(2)}) copy-start(bf16[512,512]{1,0:T(8,128)(2,1)} %param.10) | copy-start | bytes 1572868
  115.7 23.8 %all-to-all-start.1 = ((bf16[64,8,256]{2,1,0:T(8,128)(2,1)}), bf16[64,8,256]{2,1,0:T(8,128)(2,1)S(1)}, u32[]{:S(2)}, u32[]{:S(2)}) async-start(bf16[64,8,256]{2,1,0:T(8,128)(2,1)} %broadcast_select_fusion.1), calls=%async_computation.2 | async-start | bytes 524288 | tf_op jit(solution)/shard_map/all_to_all | solution.py:84
Sparse Core Ops, SparseCore 0:
  9.8 31.3 all-gather.2
  43.0 35.2 all-gather.4
  113.2 32.3 reduce-scatter.1
where the time goes:
time: 155 us
  waiting for transfers between devices  74.1 us (48%)
  matrix products  23.2 us (15%)
  starting transfers between devices  22.3 us (14%)
  between operations  15.3 us (10%)
  other arithmetic  13.9 us (9%)
  local copies, waits for them, and re-layouts  6.07 us (4%)
    all_gather x1, waiting for transfers between devices, body(): pooled = lax.all_gather(old_cache, 'tp', axis=1, tiled=True)  27.9 us
    all_gather x1, waiting for transfers between devices, body(): full_rows = lax.all_gather(tokens, 'tp', axis=1, tiled=True)  25.5 us
    all_to_all x1, waiting for transfers between devices, body(): lax.all_to_all(jnp.take(mine_part, sources, axis=0), 'seq', split_axis=0,...  13.1 us
    all_to_all x1, starting transfers between devices, body(): lax.all_to_all(pooled, 'seq', split_axis=0, concat_axis=0, tiled=True)  11.5 us
    sub x1, matrix products, body(): weights = jnp.exp(scores - top)  10.7 us
    all_to_all x1, starting transfers between devices, body(): lax.all_to_all(jnp.take(mine_part, sources, axis=0), 'seq', split_axis=0,...  10.6 us
    dot_general x1, matrix products, body(): jnp.einsum('htk,kd->thd', probs, values, preferred_element_type=jnp.float32)  7.05 us
    reduce_scatter x1, waiting for transfers between devices, body(): lax.psum_scatter(partial_out.astype(jnp.bfloat16), 'tp', scatter_dimensio...  6.08 us
  transfers between devices with their start and end apart: 5, of which 4 were waited for; matrix products, arithmetic and copies ran while one was open for 9% of the time, Pallas kernels for 0%

commit v1 on v0

--- a/solution.py
+++ b/solution.py
@@ -34,7 +34,21 @@
     groups = lax.axis_size("seq")
     tp_count = lax.axis_size("tp")
     holders = old_table[0]
-    pooled = lax.all_gather(old_cache, "tp", axis=1, tiled=True)
+    ways, here, step = (lax.axis_size("tp"), lax.axis_index("tp"), old_cache.shape[1])
+    lengths = [n * ways if d == 1 else n for d, n in enumerate(old_cache.shape)]
+    full = lax.dynamic_update_slice_in_dim(
+        jnp.zeros(lengths, old_cache.dtype), old_cache, here * step, axis=1
+    )
+    going_up = going_down = old_cache
+    for far in range(1, ways // 2 + 1):
+        going_up = lax.ppermute(going_up, "tp", [(d, (d + 1) % ways) for d in range(ways)])
+        full = lax.dynamic_update_slice_in_dim(full, going_up, (here - far) % ways * step, axis=1)
+        if 2 * far < ways:
+            going_down = lax.ppermute(going_down, "tp", [(d, (d - 1) % ways) for d in range(ways)])
+            full = lax.dynamic_update_slice_in_dim(
+                full, going_down, (here + far) % ways * step, axis=1
+            )
+    pooled = full
     arrived = lax.all_to_all(pooled, "seq", split_axis=0, concat_axis=0, tiled=True)
     ordered = jnp.take(arrived, holders, axis=0)
     block_rows = ordered.shape[1]

time: 155 us -> 139 us (0.90)
  waiting for transfers between devices: 74.1 us -> 46.9 us
  starting transfers between devices: 22.3 us -> 29.1 us
  local copies, waits for them, and re-layouts: 6.07 us -> 11.2 us
    all_gather x1 -> x0, waiting for transfers between devices: 27.9 us -> none  [body(): pooled = lax.all_gather(old_cache, 'tp', axis=1, tiled=True)]
    all_gather x1, waiting for transfers between devices: 25.5 us -> 0.02 us  [body(): full_rows = lax.all_gather(tokens, 'tp', axis=1, tiled=True)]
    all_to_all x1, waiting for transfers between devices: 0.01 us -> 24.3 us  [body(): lax.all_to_all(pooled, 'seq', split_axis=0, concat_axis=0, tiled=True)]
    ppermute x0 -> x3, starting transfers between devices: none -> 6.08 us  [the longest x2 3.98 us: body(): lax.ppermute(going_up, 'tp', [(d, (d + 1) % ways) for d in range(ways)])]
    all_to_all x1, starting transfers between devices: 11.5 us -> 16.3 us  [body(): lax.all_to_all(pooled, 'seq', split_axis=0, concat_axis=0, tiled=True)]
    ppermute x0 -> x3, waiting for transfers between devices: none -> 4.31 us  [the longest x2 4.31 us: body(): lax.ppermute(going_up, 'tp', [(d, (d + 1) % ways) for d in range(ways)])]
    all_to_all x1, starting transfers between devices: 10.6 us -> 6.45 us  [body(): lax.all_to_all(jnp.take(mine_part, sources, axis=0), 'seq', split_axis=0,...]
    dynamic_update_slice x0 -> x4, local copies, waits for them, and re-layouts: none -> 3.99 us  [the longest x1 1.7 us: body(): lax.dynamic_update_slice_in_dim(jnp.zeros(lengths, old_cache.dtype), old_...]
  transfers between devices with their start and end apart: 5 -> 7, of which waited for: 4 -> 5; matrix products, arithmetic and copies ran while one was open for 9% -> 9% of each run, Pallas kernels for 0% -> 0%
where the time goes in v1:
time: 139 us
  waiting for transfers between devices  46.9 us (34%)
  starting transfers between devices  29.1 us (21%)
  matrix products  23.2 us (17%)
  between operations  15.6 us (11%)
  other arithmetic  12.6 us (9%)
  local copies, waits for them, and re-layouts  11.2 us (8%)
    all_to_all x1, waiting for transfers between devices, body(): lax.all_to_all(pooled, 'seq', split_axis=0, concat_axis=0, tiled=True)  24.3 us
    all_to_all x1, starting transfers between devices, body(): lax.all_to_all(pooled, 'seq', split_axis=0, concat_axis=0, tiled=True)  16.3 us
    all_to_all x1, waiting for transfers between devices, body(): lax.all_to_all(jnp.take(mine_part, sources, axis=0), 'seq', split_axis=0,...  13.1 us
    sub x1, matrix products, body(): weights = jnp.exp(scores - top)  10.7 us
    dot_general x1, matrix products, body(): jnp.einsum('htk,kd->thd', probs, values, preferred_element_type=jnp.float32)  7.05 us
    all_to_all x1, starting transfers between devices, body(): lax.all_to_all(jnp.take(mine_part, sources, axis=0), 'seq', split_axis=0,...  6.45 us
    reduce_scatter x1, waiting for transfers between devices, body(): lax.psum_scatter(partial_out.astype(jnp.bfloat16), 'tp', scatter_dimensio...  5.11 us
    ppermute x2, waiting for transfers between devices, body(): lax.ppermute(going_up, 'tp', [(d, (d + 1) % ways) for d in range(ways)])  4.31 us
  transfers between devices with their start and end apart: 7, of which 5 were waited for; matrix products, arithmetic and copies ran while one was open for 9% of the time, Pallas kernels for 0%

profile of v1, /device:TPU:1, one launch (start us, length us, event | category | flops | bytes accessed | tf_op | source)
XLA Modules:
  0.0 138.6 jit_solution(15472733806858056502)
XLA Ops:
  7.2 0.0 copy-start
  7.2 0.0 all-gather.2.cloned.1.call-start
  7.2 2.2 %collective-permute-start = (bf16[64,8,256]{2,1,0:T(8,128)(2,1)}, bf16[64,8,256]{2,1,0:T(8,128)(2,1)S(1)}, u32[]{:S(2)}, u32[]{:S(2)}) collective-permute-start(bf16[64,8,256]{2,1,0:T(8,128)(2,1)} %param.19), channel_id=1, source_target_pairs={{0,1},{1,2},{2,3},{3,0},{4,5},{5,6},{6,7},{7,4},{8,9},{9,10},{10,1... | collective-permute-start | bytes 786440 | tf_op jit(solution)/shard_map/ppermute | solution.py:44
  9.4 0.0 all-gather.2.cloned.1.call-update
  9.5 2.1 %collective-permute-start.1 = (bf16[64,8,256]{2,1,0:T(8,128)(2,1)}, bf16[64,8,256]{2,1,0:T(8,128)(2,1)S(1)}, u32[]{:S(2)}, u32[]{:S(2)}) collective-permute-start(bf16[64,8,256]{2,1,0:T(8,128)(2,1)} %param.19), channel_id=1, source_target_pairs={{0,3},{1,0},{2,1},{3,2},{4,7},{5,4},{6,5},{7,6},{8,11},{9,8},{10,9... | collective-permute-start | bytes 786440 | tf_op jit(solution)/shard_map/ppermute | solution.py:47
  11.6 3.3 %collective-permute-done = bf16[64,8,256]{2,1,0:T(8,128)(2,1)S(1)} collective-permute-done((bf16[64,8,256]{2,1,0:T(8,128)(2,1)}, bf16[64,8,256]{2,1,0:T(8,128)(2,1)S(1)}, u32[]{:S(2)}, u32[]{:S(2)}) %collective-permute-start) | collective-permute-done | bytes 262176 | tf_op jit(solution)/shard_map/ppermute | solution.py:44
  14.9 1.8 %collective-permute-start.2 = (bf16[64,8,256]{2,1,0:T(8,128)(2,1)S(1)}, bf16[64,8,256]{2,1,0:T(8,128)(2,1)S(1)}, u32[]{:S(2)}, u32[]{:S(2)}) collective-permute-start(bf16[64,8,256]{2,1,0:T(8,128)(2,1)S(1)} %collective-permute-done), channel_id=1, source_target_pairs={{0,1},{1,2},{2,3},{3,0},{4,5},{5,6},{6,7},{7,4},{8,9},{9,10},{10,1... | collective-permute-start | bytes 786440 | tf_op jit(solution)/shard_map/ppermute | solution.py:44
  16.6 1.1 broadcast_in_dim.76
  17.8 1.7 %constant_dynamic-update-slice_fusion.3 = bf16[64,32,256]{2,1,0:T(8,128)(2,1)} fusion(bf16[64,32,256]{2,1,0:T(8,128)(2,1)} %broadcast_in_dim.76, bf16[64,8,256]{2,1,0:T(8,128)(2,1)} %param.19, s32[]{:T(128)S(6)} %select_n.88), kind=kLoop, calls=%fused_computation.49 | loop fusion | bytes 524292 | tf_op jit(solution)/shard_map/dynamic_update_slice | solution.py:39
  19.5 0.8 constant_dynamic-update-slice_fusion.2
  20.3 0.0 collective-permute-done.1
  20.3 0.7 constant_dynamic-update-slice_fusion.1
  21.0 1.0 collective-permute-done.2
  22.0 0.8 constant_dynamic-update-slice_fusion
  22.8 16.3 %all-to-all-start = ((bf16[64,32,256]{2,1,0:T(8,128)(2,1)}), bf16[64,32,256]{2,1,0:T(8,128)(2,1)S(1)}, u32[]{:S(2)}, u32[]{:S(2)}) async-start(bf16[64,32,256]{2,1,0:T(8,128)(2,1)} %constant_dynamic-update-slice_fusion), calls=%async_computation | async-start | bytes 2097152 | tf_op jit(solution)/shard_map/all_to_all | solution.py:52
  39.1 0.2 reduce-scatter.2.cloned.1.call-start
  39.3 0.0 copy-done.8
  39.3 0.1 select_reduce_fusion
  39.4 0.1 broadcast_in_dim.73
  39.5 0.1 broadcast_in_dim.74
  41.0 1.8 %iota_compare_fusion = pred[512,2048]{0,1:T(8,128)(4,1)} fusion(s32[512]{0:T(512)S(1)} %iota_add_fusion), kind=kLoop, calls=%fused_computation.18 | loop fusion | flops 1048576 | bytes 1050624 | tf_op jit(solution)/shard_map/le | solution.py:80
  42.8 24.3 %all-to-all-done = bf16[64,32,256]{2,1,0:T(8,128)(2,1)S(1)} async-done(((bf16[64,32,256]{2,1,0:T(8,128)(2,1)}), bf16[64,32,256]{2,1,0:T(8,128)(2,1)S(1)}, u32[]{:S(2)}, u32[]{:S(2)}) %all-to-all-start) | async-done | bytes 1048608 | tf_op jit(solution)/shard_map/all_to_all | solution.py:52
  67.1 1.6 %gather_fusion = bf16[64,32,256]{2,1,0:T(8,128)(2,1)} fusion(bf16[64,32,256]{2,1,0:T(8,128)(2,1)S(1)} %all-to-all-done, s32[1024]{0:T(1024)S(1)} %pad_clamp_fusion.1), kind=kCustom, calls=%fused_computation | custom fusion | bytes 2097408 | tf_op jit(solution)/shard_map/jit(_take)/gather | solution.py:53
  68.7 1.5 %bitcast_select_fusion.4 = bf16[2048,256]{1,0:T(8,128)(2,1)S(1)} fusion(bf16[64,32,256]{2,1,0:T(8,128)(2,1)} %gather_fusion, pred[2048]{0:T(1024)(128)(4,1)S(1)} %broadcast_in_dim.74), kind=kLoop, calls=%fused_computation.24 | loop fusion | flops 524288 | bytes 2099200 | tf_op jit(solution)/shard_map/jit(_take)/select_n | solution.py:53
  70.2 0.0 all-gather.2.cloned.1.call-done
  70.2 0.0 copy-start.7
  70.2 2.1 %convert_reduce_fusion = f32[512]{0:T(512)S(1)} fusion(bf16[512,2048]{1,0:T(8,128)(2,1)} %all-gather.2.cloned.1.call-done), kind=kLoop, calls=%fused_computation.12 | loop fusion | flops 2096640 | bytes 2099200 | tf_op jit(solution)/shard_map/reduce_sum | solution.py:12
  72.3 2.3 %fusion.8 = f32[512]{0:T(512)S(1)} fusion(bf16[512,2048]{1,0:T(8,128)(2,1)} %all-gather.2.cloned.1.call-done, f32[512]{0:T(512)S(1)} %broadcast_multiply_fusion), kind=kLoop, calls=%fused_computation.15 | loop fusion | flops 4193792 | bytes 2101248 | tf_op jit(solution)/shard_map/reduce_sum | solution.py:14
  74.6 0.7 fusion.10
  75.3 0.7 convolution_convert_fusion.2
  76.1 0.1 copy-done.6
  76.2 2.1 %convolution_convert_fusion.1 = bf16[512,512]{0,1:T(8,128)(2,1)} fusion(bf16[512,2048]{1,0:T(8,128)(2,1)S(1)} %fusion.10, bf16[2048,512]{1,0:T(8,128)(2,1)S(1)} %copy-done.6), kind=kOutput, calls=%fused_computation.21 | convolution fusion | flops 1074003968 | bytes 4718592 | tf_op jit(solution)/shard_map/dot_general | solution.py:32
  78.3 1.8 %dynamic_update_slice.19 = bf16[2048,256]{1,0:T(8,128)(2,1)S(1)} dynamic-update-slice(bf16[2048,256]{1,0:T(8,128)(2,1)S(1)} %bitcast_select_fusion.4, bf16[512,256]{1,0:T(8,128)(2,1)S(1)} %convolution_convert_fusion.2, s32[]{:T(128)S(6)} %select_n.97, s32[]{:T(128)} %constant.64.clone.1) | dynamic-update-slice | bytes 524292 | tf_op jit(solution)/shard_map/dynamic_update_slice | solution.py:68
  80.1 1.3 broadcast_select_fusion
  81.4 10.7 %fusion.19 = (f32[4,512]{1,0:T(4,128)S(1)}, f32[4,512,2048]{1,2,0:T(8,128)}) fusion(pred[512,2048]{0,1:T(8,128)(4,1)} %iota_compare_fusion, bf16[512,4,128]{0,2,1:T(8,128)(2,1)} %bitcast.63, bf16[2048,256]{1,0:T(8,128)(2,1)} %broadcast_select_fusion), kind=kOutput, calls=%fused_computation.55 | convolution fusion | flops 1090521088 | bytes 18882560 | tf_op jit(solution)/shard_map/sub | solution.py:83
  92.1 0.0 copy-done.3
  92.1 7.0 %fusion.13 = bf16[128,4,512]{2,0,1:T(8,128)(2,1)S(1)} fusion(f32[4,512,2048]{1,2,0:T(8,128)} %get-tuple-element.3, f32[4,512]{1,0:T(4,128)S(1)} %get-tuple-element.2, bf16[2048,256]{1,0:T(8,128)(2,1)S(1)} %copy-done.3), kind=kOutput, calls=%fused_computation.22 | convolution fusion | flops 1082392576 | bytes 17833984 | tf_op jit(solution)/shard_map/htk,kd->thd/dot_general | solution.py:85
  99.2 0.0 copy-start.2
  99.2 2.6 %convolution_convert_fusion = bf16[512,2048]{1,0:T(8,128)(2,1)} fusion(bf16[512,512]{0,1:T(8,128)(2,1)S(1)} %bitcast.64, bf16[512,2048]{1,0:T(8,128)(2,1)S(1)} %copy-done), kind=kOutput, calls=%fused_computation.19 | convolution fusion | flops 1074790400 | bytes 4718592 | tf_op jit(solution)/shard_map/dot_general | solution.py:89
  101.8 0.0 reduce-scatter.2.cloned.1.call-update
  101.9 1.0 constant_dynamic-slice_fusion
  102.8 0.6 gather_fusion.1
  103.5 0.8 broadcast_select_fusion.1
  104.3 6.4 %all-to-all-start.1 = ((bf16[64,8,256]{2,1,0:T(8,128)(2,1)}), bf16[64,8,256]{2,1,0:T(8,128)(2,1)S(1)}, u32[]{:S(2)}, u32[]{:S(2)}) async-start(bf16[64,8,256]{2,1,0:T(8,128)(2,1)} %broadcast_select_fusion.1), calls=%async_computation.2 | async-start | bytes 524288 | tf_op jit(solution)/shard_map/all_to_all | solution.py:98
  110.8 13.1 %all-to-all-done.1 = bf16[64,8,256]{2,1,0:T(8,128)(2,1)S(1)} async-done(((bf16[64,8,256]{2,1,0:T(8,128)(2,1)}), bf16[64,8,256]{2,1,0:T(8,128)(2,1)S(1)}, u32[]{:S(2)}, u32[]{:S(2)}) %all-to-all-start.1) | async-done | bytes 262176 | tf_op jit(solution)/shard_map/all_to_all | solution.py:98
  123.9 5.1 %reduce-scatter.2.cloned.1.call-done = bf16[512,512]{1,0:T(8,128)(2,1)} async-done(((bf16[512,2048]{1,0:T(8,128)(2,1)}), bf16[512,512]{1,0:T(8,128)(2,1)}) %reduce-scatter.2.cloned.1.call-update) | async-done | bytes 524304 | tf_op jit(solution)/shard_map/reduce_scatter | solution.py:90
  129.0 2.0 %select_convert_fusion = bf16[512,512]{1,0:T(8,128)(2,1)} fusion(bf16[512,512]{1,0:T(8,128)(2,1)} %reduce-scatter.2.cloned.1.call-done, bf16[512,512]{1,0:T(8,128)(2,1)S(1)} %copy-done.2, pred[512]{0:T(512)(128)(4,1)S(1)} %iota_compare_fusion.3), kind=kLoop, calls=%fused_computation.25 | loop fusion | flops 1310720 | bytes 1573376 | tf_op jit(solution)/shard_map/convert_element_type | solution.py:94
  131.0 0.7 copy.33
  (22 shorter events, 0.1 us)
Async XLA Ops:
  7.2 92.0 %copy-start = (bf16[512,2048]{1,0:T(8,128)(2,1)S(1)}, bf16[512,2048]{1,0:T(8,128)(2,1)}, u32[]{:S(2)}) copy-start(bf16[512,2048]{1,0:T(8,128)(2,1)} %param.14) | copy-start | bytes 6291460
  7.2 32.1 %copy-start.8 = (s32[1,64]{1,0:T(1,128)S(1)}, s32[1,64]{1,0:T(1,128)}, u32[]{:S(2)}) copy-start(s32[1,64]{1,0:T(1,128)} %param.18) | copy-start | bytes 772
  7.2 32.2 %copy-start.5 = (s32[1,64]{1,0:T(1,128)S(1)}, s32[1,64]{1,0:T(1,128)}, u32[]{:S(2)}) copy-start(s32[1,64]{1,0:T(1,128)} %param.17) | copy-start | bytes 772
  7.2 63.0 %all-gather.2.cloned.1.call-start = ((), (), s32[]{:S(2)}) async-start(), calls=%async_computation.3 | async-start | bytes 2621440 | tf_op jit(solution)/shard_map/all_gather | solution.py:30
  7.2 7.6 %collective-permute-start = (bf16[64,8,256]{2,1,0:T(8,128)(2,1)}, bf16[64,8,256]{2,1,0:T(8,128)(2,1)S(1)}, u32[]{:S(2)}, u32[]{:S(2)}) collective-permute-start(bf16[64,8,256]{2,1,0:T(8,128)(2,1)} %param.19), channel_id=1, source_target_pairs={{0,1},{1,2},{2,3},{3,0},{4,5},{5,6},{6,7},{7,4},{8,9},{9,10},{10,1... | collective-permute-start | bytes 786440 | tf_op jit(solution)/shard_map/ppermute | solution.py:44
  9.5 10.8 %collective-permute-start.1 = (bf16[64,8,256]{2,1,0:T(8,128)(2,1)}, bf16[64,8,256]{2,1,0:T(8,128)(2,1)S(1)}, u32[]{:S(2)}, u32[]{:S(2)}) collective-permute-start(bf16[64,8,256]{2,1,0:T(8,128)(2,1)} %param.19), channel_id=1, source_target_pairs={{0,3},{1,0},{2,1},{3,2},{4,7},{5,4},{6,5},{7,6},{8,11},{9,8},{10,9... | collective-permute-start | bytes 786440 | tf_op jit(solution)/shard_map/ppermute | solution.py:47
  14.9 7.2 %collective-permute-start.2 = (bf16[64,8,256]{2,1,0:T(8,128)(2,1)S(1)}, bf16[64,8,256]{2,1,0:T(8,128)(2,1)S(1)}, u32[]{:S(2)}, u32[]{:S(2)}) collective-permute-start(bf16[64,8,256]{2,1,0:T(8,128)(2,1)S(1)} %collective-permute-done), channel_id=1, source_target_pairs={{0,1},{1,2},{2,3},{3,0},{4,5},{5,6},{6,7},{7,4},{8,9},{9,10},{10,1... | collective-permute-start | bytes 786440 | tf_op jit(solution)/shard_map/ppermute | solution.py:44
  22.8 44.3 %all-to-all-start = ((bf16[64,32,256]{2,1,0:T(8,128)(2,1)}), bf16[64,32,256]{2,1,0:T(8,128)(2,1)S(1)}, u32[]{:S(2)}, u32[]{:S(2)}) async-start(bf16[64,32,256]{2,1,0:T(8,128)(2,1)} %constant_dynamic-update-slice_fusion), calls=%async_computation | async-start | bytes 2097152 | tf_op jit(solution)/shard_map/all_to_all | solution.py:52
  39.1 90.0 %reduce-scatter.2.cloned.1.call-start = ((), (), s32[]{:S(2)}) async-start(), calls=%async_computation.4 | async-start | bytes 2621440 | tf_op jit(solution)/shard_map/reduce_scatter | solution.py:90
  42.8 31.8 %copy-start.4 = (f32[2048]{0:T(1024)S(1)}, f32[2048]{0:T(1024)}, u32[]{:S(2)}) copy-start(f32[2048]{0:T(1024)} %param.11) | copy-start | bytes 24580
  70.2 4.4 %copy-start.1 = (bf16[512,2048]{1,0:T(8,128)(2,1)S(1)}, bf16[512,2048]{1,0:T(8,128)(2,1)}, u32[]{:S(2)}) copy-start(bf16[512,2048]{1,0:T(8,128)(2,1)} %all-gather.2.cloned.1.call-done) | copy-start | bytes 6291460
  70.2 5.1 %copy-start.7 = (bf16[2048,256]{1,0:T(8,128)(2,1)S(1)}, bf16[2048,256]{1,0:T(8,128)(2,1)}, u32[]{:S(2)}) copy-start(bf16[2048,256]{1,0:T(8,128)(2,1)} %param.13) | copy-start | bytes 3145732
  74.6 1.6 %copy-start.6 = (bf16[2048,512]{1,0:T(8,128)(2,1)S(1)}, bf16[2048,512]{1,0:T(8,128)(2,1)}, u32[]{:S(2)}) copy-start(bf16[2048,512]{1,0:T(8,128)(2,1)} %param.12) | copy-start | bytes 6291460
  81.4 10.7 %copy-start.3 = (bf16[2048,256]{1,0:T(8,128)(2,1)S(1)}, bf16[2048,256]{1,0:T(8,128)(2,1)}, u32[]{:S(2)}) copy-start(bf16[2048,256]{1,0:T(8,128)(2,1)} %broadcast_select_fusion) | copy-start | bytes 3145732
  99.2 29.9 %copy-start.2 = (bf16[512,512]{1,0:T(8,128)(2,1)S(1)}, bf16[512,512]{1,0:T(8,128)(2,1)}, u32[]{:S(2)}) copy-start(bf16[512,512]{1,0:T(8,128)(2,1)} %param.10) | copy-start | bytes 1572868
  104.3 19.6 %all-to-all-start.1 = ((bf16[64,8,256]{2,1,0:T(8,128)(2,1)}), bf16[64,8,256]{2,1,0:T(8,128)(2,1)S(1)}, u32[]{:S(2)}, u32[]{:S(2)}) async-start(bf16[64,8,256]{2,1,0:T(8,128)(2,1)} %broadcast_select_fusion.1), calls=%async_computation.2 | async-start | bytes 524288 | tf_op jit(solution)/shard_map/all_to_all | solution.py:98
Sparse Core Ops, SparseCore 0:
  9.8 37.2 all-gather.1
  102.0 27.0 reduce-scatter.1
